TPU v7x, 32 devices: a whole 2x2x4 slice. The times are simulated.
32 devices in a mesh: row: 2 (over core), col: 4 (over z), kk: 4 (over y, x).
Axes of the slice: x: 2, y: 2, z: 4, core: 2. Of those that a mesh axis runs over, the one named last changes fastest.
Arguments:
- contribution: float32 [32, 256, 16, 512], P('kk', 'row', None, 'col'), may hold values from -6 to 6
- left_panel: float32 [32, 256, 4, 768], P(None, 'row', 'kk', 'col'), may hold values from -6 to 6
- right_panel: float32 [4, 768, 16, 512], P('kk', 'row', None, 'col'), may hold values from -0.109375 to 0.109375
Outputs:
- updated: float32 [32, 256, 16, 512], P('kk', 'row', None, 'col')
All inputs are finite; a program needn't handle non-finite values.
Results may differ from a plain program's by a relative error of at most 0.00005.
Values sent between devices are 32-bit elements; how exact they have to be, the bound alone decides.
No kernel may reach another device: no remote copies, remote signals or barrier semaphores. Data moves between devices by JAX's collectives and lax.ppermute only.
A program may use at most 128 MiB of HBM per device.

v0:
```python
import jax
import jax.numpy as jnp
from jax import lax
from jax.sharding import PartitionSpec as P


def local(contribution, left_panel, right_panel):
    right_rows = lax.all_gather(right_panel, "row", axis=1, tiled=True)
    col_width = contribution.shape[2] * contribution.shape[3]
    exchanged = lax.all_to_all(left_panel, "kk", split_axis=0, concat_axis=2, tiled=True)
    left_full = lax.all_gather(exchanged, "col", axis=3, tiled=True)
    right_full = lax.all_gather(right_rows, "kk", axis=0, tiled=True)
    row_total = left_full.shape[0] * left_full.shape[1]
    left_flat = left_full.reshape(row_total, -1)
    right_flat = right_full.reshape(-1, col_width)
    product = jnp.dot(
        left_flat, right_flat, precision=lax.Precision.HIGHEST, preferred_element_type=jnp.float32
    )
    product = product.reshape(contribution.shape)
    return contribution - product


def solution(mesh):
    placed = (P("kk", "row", None, "col"), P(None, "row", "kk", "col"), P("kk", "row", None, "col"))
    return jax.shard_map(
        local, mesh=mesh, in_specs=placed, out_specs=P("kk", "row", None, "col"), check_vma=False
    )
```

profile of v0, /device:TPU:0, one launch (start us, length us, event | category | flops | bytes accessed | tf_op | source)
XLA Modules:
  0.0 655.1 jit_solution(10757515280889346965)
XLA Ops:
  6.5 0.0 all-gather.5.cloned.1.call-start
  6.5 0.7 all-gather.5.cloned.1.call-update
  7.3 0.0 all-gather.9.cloned.1.call-start
  7.3 41.9 %all_to_all.18 = f32[32,128,1,192]{1,3,2,0:T(8,128)S(1)} all-to-all(f32[32,128,1,192]{1,3,2,0:T(8,128)} %param.4), channel_id=1, replica_groups=mesh['row'=2,'col'=4,'kk'=4] {'kk'}, dimensions={0} | all-to-all | bytes 6291456 | tf_op jit(solution)/shard_map/all_to_all | solution.py:10
  49.2 3.5 copy.21
  52.6 0.0 all-gather.9.cloned.1.call-update
  52.7 0.0 all-gather.7.cloned.1.call-start
  52.7 0.0 all-gather.5.cloned.1.call-done
  52.7 0.7 all-gather.7.cloned.1.call-update
  53.4 217.5 %all-gather.9.cloned.1.call-done = f32[8,128,4,1,768]{1,0,3,2,4:T(8,128)} async-done(((f32[8,128,4,1,192]{1,0,3,2,4:T(8,128)}), f32[8,128,4,1,768]{1,0,3,2,4:T(8,128)}) %all-gather.9.cloned.1.call-update) | async-done | bytes 12582928 | tf_op jit(solution)/shard_map/all_gather | solution.py:11
  270.9 14.2 %copy.9 = f32[8,128,4,1,768]{4,2,1,0,3:T(4,128)} copy(f32[8,128,4,1,768]{1,0,3,2,4:T(8,128)} %all-gather.9.cloned.1.call-done) | data formatting | bytes 25165824 | tf_op jit(solution)/shard_map/all_gather | solution.py:11
  285.1 16.0 %reshape.11 = f32[8,128,3072,1]{2,1,0,3:T(8,128)} reshape(f32[8,128,4,1,768]{4,2,1,0,3:T(4,128)} %copy.9) | data formatting | bytes 25165824 | tf_op jit(solution)/shard_map/dot_general | solution.py:16
  301.1 197.5 %all-gather.7.cloned.1.call-done = f32[4,768,16,128]{3,2,1,0:T(8,128)} async-done(((f32[1,768,16,128]{3,2,1,0:T(8,128)}), f32[4,768,16,128]{3,2,1,0:T(8,128)}) %all-gather.7.cloned.1.call-update) | async-done | bytes 25165840 | tf_op jit(solution)/shard_map/all_gather | solution.py:12
  498.6 22.8 %copy.20 = f32[384,8,16,128]{3,1,2,0:T(8,128)} copy(f32[384,8,16,128]{3,2,1,0:T(8,128)} %bitcast.26) | data formatting | bytes 50331648
  521.4 24.8 %copy.12 = f32[3072,2048]{0,1:T(8,128)} copy(f32[3072,2048]{1,0:T(8,128)} %bitcast.25) | data formatting | bytes 50331648 | tf_op jit(solution)/shard_map/reshape | solution.py:15
  546.2 90.9 %copy_subtract_fusion = f32[8,128,16,128]{3,1,2,0:T(8,128)} fusion(f32[8,128,16,128]{3,2,1,0:T(8,128)} %param.3, f32[16,128,3072,1]{2,1,0,3:T(8,128)} %bitcast.27, f32[8,128,3072,1]{2,1,0,3:T(8,128)} %reshape.11), kind=kOutput, calls=%fused_computation.3 | convolution fusion | flops 77311508480 | bytes 54525952 | tf_op jit(solution)/shard_map/dot_general | solution.py:16
  637.0 11.5 %copy.14 = f32[8,128,16,128]{3,2,1,0:T(8,128)} copy(f32[8,128,16,128]{3,1,2,0:T(8,128)} %copy_subtract_fusion) | data formatting | bytes 16777216 | tf_op jit(solution)/shard_map/sub | solution.py:20
Async XLA Ops:
  6.5 46.2 %all-gather.5.cloned.1.call-start = ((), (), s32[]{:S(2)}) async-start(), calls=%async_computation.1 | async-start | bytes 9437184 | tf_op jit(solution)/shard_map/all_gather | solution.py:8
  7.3 263.7 %all-gather.9.cloned.1.call-start = ((), (), s32[]{:S(2)}) async-start(), calls=%async_computation.3 | async-start | bytes 15728640 | tf_op jit(solution)/shard_map/all_gather | solution.py:11
  52.7 445.9 %all-gather.7.cloned.1.call-start = ((), (), s32[]{:S(2)}) async-start(), calls=%async_computation.2 | async-start | bytes 31457280 | tf_op jit(solution)/shard_map/all_gather | solution.py:12
Sparse Core Ops, SparseCore 0:
  8.9 19.4 all-gather.4
  52.8 218.0 all-gather.8
  272.8 225.7 all-gather.6
where the time goes:
time: 656 us; the launch traced here: 655 us
  waiting for transfers between devices  416 us (63%)
  local copies, waits for them, and re-layouts  92.8 us (14%)
  matrix products  90.9 us (14%)
  blocking collectives  41.9 us (6%)
  between operations  13.1 us (2%)
    all_gather x1, waiting for transfers between devices, local(): left_full = lax.all_gather(exchanged, 'col', axis=3, tiled=True)  218 us
    all_gather x1, waiting for transfers between devices, local(): right_full = lax.all_gather(right_rows, 'kk', axis=0, tiled=True)  197 us
    dot_general x1, matrix products, local(): jnp.dot(left_flat, right_flat, precision=lax.Precision.HIGHEST, preferred...  90.9 us
    all_to_all x1, blocking collectives, local(): lax.all_to_all(left_panel, 'kk', split_axis=0, concat_axis=2, tiled=True)  41.9 us
    reshape x1, local copies, waits for them, and re-layouts, local(): right_flat = right_full.reshape(-1, col_width)  24.8 us
    unnamed x1, local copies, waits for them, and re-layouts  22.8 us
    dot_general x1, local copies, waits for them, and re-layouts, local(): jnp.dot(left_flat, right_flat, precision=lax.Precision.HIGHEST, preferred...  16 us
    all_gather x1, local copies, waits for them, and re-layouts, local(): left_full = lax.all_gather(exchanged, 'col', axis=3, tiled=True)  14.2 us
  transfers between devices with their start and end apart: 3, of which 2 were waited for; matrix products, arithmetic and copies ran while one was open for 5% of the time, Pallas kernels for 0%

commit v1 on v0

--- a/solution.py
+++ b/solution.py
@@ -8,7 +8,9 @@
     right_rows = lax.all_gather(right_panel, "row", axis=1, tiled=True)
     col_width = contribution.shape[2] * contribution.shape[3]
     exchanged = lax.all_to_all(left_panel, "kk", split_axis=0, concat_axis=2, tiled=True)
-    left_full = lax.all_gather(exchanged, "col", axis=3, tiled=True)
+    left_full = jnp.concatenate(
+        lax.all_to_all(jnp.stack([exchanged] * lax.axis_size("col")), "col", 0, 0), axis=3
+    )
     right_full = lax.all_gather(right_rows, "kk", axis=0, tiled=True)
     row_total = left_full.shape[0] * left_full.shape[1]
     left_flat = left_full.reshape(row_total, -1)

time: 656 us -> 613 us (0.934)
  waiting for transfers between devices: 416 us -> 21.8 us
  blocking collectives: 41.9 us -> 338 us
  matrix products: 90.9 us -> 167 us
  local copies, waits for them, and re-layouts: 92.8 us -> 71.6 us
    all_to_all x0 -> x1, blocking collectives: none -> 276 us  [local(): lax.all_to_all(jnp.stack([exchanged] * lax.axis_size('col')), 'col', 0, 0)]
    all_gather x1 -> x0, waiting for transfers between devices: 218 us -> none  [local(): left_full = lax.all_gather(exchanged, 'col', axis=3, tiled=True)]
    all_gather x1, waiting for transfers between devices: 197 us -> 0.01 us  [local(): right_full = lax.all_gather(right_rows, 'kk', axis=0, tiled=True)]
    dot_general x1, matrix products: 90.9 us -> 167 us  [local(): jnp.dot(left_flat, right_flat, precision=lax.Precision.HIGHEST, preferred...]
    all_gather x1, waiting for transfers between devices: 0.02 us -> 21.1 us  [local(): right_rows = lax.all_gather(right_panel, 'row', axis=1, tiled=True)]
    all_to_all x1, blocking collectives: 41.9 us -> 62.1 us  [local(): lax.all_to_all(left_panel, 'kk', split_axis=0, concat_axis=2, tiled=True)]
    dot_general x1 -> x0, local copies, waits for them, and re-layouts: 16 us -> none  [local(): jnp.dot(left_flat, right_flat, precision=lax.Precision.HIGHEST, preferred...]
    all_gather x1 -> x0, local copies, waits for them, and re-layouts: 14.2 us -> none  [local(): left_full = lax.all_gather(exchanged, 'col', axis=3, tiled=True)]
  transfers between devices with their start and end apart: 3 -> 2, of which waited for: 2 -> 1; matrix products, arithmetic and copies ran while one was open for 5% -> 2% of each run, Pallas kernels for 0% -> 0%
where the time goes in v1:
time: 613 us; the launch traced here: 612 us
  blocking collectives  338 us (55%)
  matrix products  167 us (27%)
  local copies, waits for them, and re-layouts  71.6 us (12%)
  waiting for transfers between devices  21.8 us (4%)
  between operations  13.4 us (2%)
    all_to_all x1, blocking collectives, local(): lax.all_to_all(jnp.stack([exchanged] * lax.axis_size('col')), 'col', 0, 0)  276 us
    dot_general x1, matrix products, local(): jnp.dot(left_flat, right_flat, precision=lax.Precision.HIGHEST, preferred...  167 us
    all_to_all x1, blocking collectives, local(): lax.all_to_all(left_panel, 'kk', split_axis=0, concat_axis=2, tiled=True)  62.1 us
    reshape x1, local copies, waits for them, and re-layouts, local(): right_flat = right_full.reshape(-1, col_width)  24.7 us
    unnamed x1, local copies, waits for them, and re-layouts  22.8 us
    all_gather x1, waiting for transfers between devices, local(): right_rows = lax.all_gather(right_panel, 'row', axis=1, tiled=True)  21.1 us
  transfers between devices with their start and end apart: 2, of which 1 were waited for; matrix products, arithmetic and copies ran while one was open for 2% of the time, Pallas kernels for 0%

profile of v1, /device:TPU:0, one launch (start us, length us, event | category | flops | bytes accessed | tf_op | source)
XLA Modules:
  0.0 611.8 jit_solution(6363126512765457398)
XLA Ops:
  6.5 0.0 all-gather.3.cloned.1.call-start
  6.5 0.7 all-gather.3.cloned.1.call-update
  7.3 0.0 all-gather.5.cloned.1.call-start
  7.3 21.1 %all-gather.3.cloned.1.call-done = f32[1,768,16,128]{3,2,0,1:T(8,128)} async-done(((f32[1,384,16,128]{3,2,0,1:T(8,128)}), f32[1,768,16,128]{3,2,0,1:T(8,128)}) %all-gather.3.cloned.1.call-update) | async-done | bytes 6291472 | tf_op jit(solution)/shard_map/all_gather | solution.py:8
  28.4 0.0 all-gather.5.cloned.1.call-update
  28.4 62.1 %all_to_all.20 = f32[32,128,1,192]{1,3,2,0:T(8,128)S(1)} all-to-all(f32[32,128,1,192]{1,3,2,0:T(8,128)} %param.4), channel_id=1, replica_groups=mesh['row'=2,'col'=4,'kk'=4] {'kk'}, dimensions={0} | all-to-all | bytes 6291456 | tf_op jit(solution)/shard_map/all_to_all | solution.py:10
  90.5 0.3 copy.29
  90.9 1.6 stack.10
  92.4 276.0 %all_to_all.21 = f32[4,8,128,4,192]{2,4,3,1,0:T(8,128)} all-to-all(f32[4,8,128,4,192]{2,4,3,1,0:T(8,128)S(1)} %stack.10), channel_id=1, replica_groups=mesh['row'=2,'col'=4,'kk'=4] {'col'}, dimensions={0} | all-to-all | bytes 25165824 | tf_op jit(solution)/shard_map/all_to_all | solution.py:12
  368.5 10.7 %copy.14 = f32[4,8,128,4,192]{2,4,0,3,1:T(8,128)} copy(f32[4,8,128,4,192]{2,4,3,1,0:T(8,128)} %all_to_all.21) | data formatting | bytes 25165824 | tf_op jit(solution)/shard_map/all_to_all | solution.py:12
  379.2 0.0 all-gather.5.cloned.1.call-done
  379.2 22.8 %copy.28 = f32[384,8,16,128]{3,1,2,0:T(8,128)} copy(f32[384,8,16,128]{3,2,1,0:T(8,128)} %bitcast.28) | data formatting | bytes 50331648
  402.0 24.7 %copy.17 = f32[3072,2048]{0,1:T(8,128)} copy(f32[3072,2048]{1,0:T(8,128)} %bitcast.27) | data formatting | bytes 50331648 | tf_op jit(solution)/shard_map/reshape | solution.py:17
  426.7 166.8 %copy_subtract_fusion = f32[8,128,16,128]{3,1,2,0:T(8,128)} fusion(f32[8,128,16,128]{3,2,1,0:T(8,128)} %param.3, f32[8,128,3072,1]{1,2,3,0:T(8,128)} %bitcast.30, f32[16,128,3072,1]{2,1,0,3:T(8,128)} %bitcast.29), kind=kOutput, calls=%fused_computation.1 | convolution fusion | flops 77311508480 | bytes 54525952 | tf_op jit(solution)/shard_map/dot_general | solution.py:18
  593.5 11.5 %copy.20 = f32[8,128,16,128]{3,2,1,0:T(8,128)} copy(f32[8,128,16,128]{3,1,2,0:T(8,128)} %copy_subtract_fusion) | data formatting | bytes 16777216 | tf_op jit(solution)/shard_map/sub | solution.py:22
Async XLA Ops:
  6.5 21.8 %all-gather.3.cloned.1.call-start = ((), (), s32[]{:S(2)}) async-start(), calls=%async_computation.2 | async-start | bytes 9437184 | tf_op jit(solution)/shard_map/all_gather | solution.py:8
  7.3 371.9 %all-gather.5.cloned.1.call-start = ((), (), s32[]{:S(2)}) async-start(), calls=%async_computation.3 | async-start | bytes 31457280 | tf_op jit(solution)/shard_map/all_gather | solution.py:14
Sparse Core Ops, SparseCore 0:
  8.9 19.4 all-gather.2
  30.2 248.9 all-gather.4
